TPU v7x, 256 devices: a whole 4x4x8 slice. The times are simulated.
256 devices in a mesh: span: 4 (over y), ty: 8 (over z_hi, core), tx: 8 (over z_lo, x).
Axes of the slice: x: 4, y: 4, z: 8 (z_hi: 4, z_lo: 2; z = z_hi * 2 + z_lo), core: 2. Of those that a mesh axis runs over, the one named last changes fastest.
Arguments:
- queries: bfloat16 [4, 8, 8, 128, 1536], P('span', 'ty', 'tx'), may hold values from -125 to 125
- key_value: bfloat16 [4, 8, 8, 128, 1024], P('span', 'ty', 'tx'), may hold values from -5 to 5
- pattern: int32 [4, 8, 8, 5], P('span', 'ty', 'tx'), may hold values from 0 to 1
- counts: int32 [4, 8, 8], replicated, may hold values from 64 to 128, as said below
- span_mask: int32 [4, 4], replicated, may hold values from 0 to 1, as said below
Outputs:
- attended: bfloat16 [4, 8, 8, 128, 1536], P('span', 'ty', 'tx')
Inputs may be any that keep to these rules, and one draw needn't show every extreme that they name: `counts`: in every span some tile has all 128 slots valid. span_mask[c, c] is 1 and span_mask[c, c'] is 0 for c' > c.
All inputs are finite; a program needn't handle non-finite values.
Results may differ from a plain program's by a relative error of at most 0.006.
Values may be sent and summed in bfloat16 or wider, within the bound.
A program may use at most 64 MiB of HBM per device.

v0:
```python
import jax
import jax.numpy as jnp
from jax import lax
from jax.sharding import PartitionSpec as P

HEAD_SIZE = 128
NEIGH = 5


def padded(block, sides, width):
    for axis, dim in sides:
        count = lax.axis_size(axis)
        forward = [(i, i + 1) for i in range(count - 1)]
        backward = [(target, source) for source, target in forward]
        low = lax.ppermute(
            lax.slice_in_dim(block, block.shape[dim] - width, None, axis=dim), axis, forward
        )
        high = lax.ppermute(lax.slice_in_dim(block, 0, width, axis=dim), axis, backward)
        block = jnp.concatenate([low, block, high], axis=dim)
    return block


def cross_tiles(extended):
    return jnp.stack(
        [
            extended[:, 1, 1],
            extended[:, 0, 1],
            extended[:, 2, 1],
            extended[:, 1, 0],
            extended[:, 1, 2],
        ],
        axis=1,
    )


def shards(queries, key_value, pattern, counts, span_mask):
    tok_rows = queries.shape[3]
    kv_width = key_value.shape[4] // 2
    kv_heads = kv_width // HEAD_SIZE
    groups = queries.shape[4] // kv_width
    scale = HEAD_SIZE ** (-0.5)
    my_span = lax.axis_index("span")
    my_row = lax.axis_index("ty")
    my_col = lax.axis_index("tx")
    zero_index = jnp.asarray(0).astype(jnp.int32)
    padded_counts = jnp.pad(counts, ((0, 0), (1, 1), (1, 1)))
    window = lax.dynamic_slice(padded_counts, (zero_index, my_row, my_col), (counts.shape[0], 3, 3))
    near_counts = cross_tiles(window)
    own_count = lax.dynamic_index_in_dim(window[:, 1, 1], my_span, 0, keepdims=False)
    allowed = pattern.reshape(NEIGH) > 0
    span_row = lax.dynamic_index_in_dim(span_mask, my_span, 0, keepdims=False) > 0
    query_rows = queries.reshape(tok_rows, kv_heads, groups, HEAD_SIZE)
    row_ids = jnp.arange(tok_rows, dtype=jnp.int32)
    initial = (
        jnp.full((tok_rows, kv_heads, groups), -1e30, jnp.float32),
        jnp.zeros((tok_rows, kv_heads, groups), jnp.float32),
        jnp.zeros((tok_rows, kv_heads, groups, HEAD_SIZE), jnp.float32),
    )
    cached = lax.all_gather(key_value, "span", axis=0, tiled=True)
    extended = padded(cached, (("ty", 1), ("tx", 2)), 1)
    state_now = initial
    kv_piece = cross_tiles(extended)
    for offset in range(kv_piece.shape[0]):
        key_value_block = kv_piece[offset]
        source_span = 0 + offset
        attend_run_max, attend_run_sum, attend_accumulated = state_now
        key_matrix = key_value_block[:, :, :kv_width].reshape(-1, kv_heads, HEAD_SIZE)
        value_rows = key_value_block[:, :, kv_width:].reshape(-1, kv_heads, HEAD_SIZE)
        near_count = lax.dynamic_index_in_dim(near_counts, source_span, 0, keepdims=False)
        open_span = lax.dynamic_index_in_dim(span_row, source_span, 0, keepdims=False)
        live_keys = (
            (row_ids[None, :] < near_count[:, None]) & allowed[:, None] & open_span
        ).reshape(-1)
        scores = (
            jnp.einsum("tkgd,lkd->tkgl", query_rows, key_matrix, preferred_element_type=jnp.float32)
            * scale
        )
        scores = jnp.where(live_keys, scores, -1e30)
        new_max = jnp.maximum(attend_run_max, jnp.max(scores, axis=-1))
        weights = jnp.where(live_keys, jnp.exp(scores - new_max[..., None]), 0.0)
        fade_factor = jnp.exp(attend_run_max - new_max)
        attend_run_sum = attend_run_sum * fade_factor + jnp.sum(weights, axis=-1)
        update = jnp.einsum(
            "tkgl,lkd->tkgd",
            weights.astype(jnp.bfloat16),
            value_rows,
            preferred_element_type=jnp.float32,
        )
        attend_accumulated = attend_accumulated * fade_factor[..., None] + update
        final_output = (new_max, attend_run_sum, attend_accumulated)
        state_now = final_output
    run_max, run_sum, accumulated = state_now
    attended = jnp.where(
        row_ids[:, None, None, None] < own_count, accumulated / run_sum[..., None], 0.0
    )
    return attended.reshape(1, 1, 1, tok_rows, -1).astype(jnp.bfloat16)


def solution(mesh):
    return jax.shard_map(
        shards,
        mesh=mesh,
        in_specs=(
            P("span", "ty", "tx", None, None),
            P("span", "ty", "tx", None, None),
            P("span", "ty", "tx", None),
            P(),
            P(),
        ),
        out_specs=P("span", "ty", "tx", None, None),
        check_vma=False,
    )
```

profile of v0, /device:TPU:70, one launch (start us, length us, event | category | flops | bytes accessed | tf_op | source)
XLA Modules:
  0.0 194.1 jit_solution(15995230202677580363)
XLA Ops:
  6.5 0.7 all-gather.2.cloned.1.call-update
  7.3 30.7 %all-gather.2.cloned.1.call-done = bf16[4,1,1,128,1024]{4,3,2,1,0:T(8,128)(2,1)} async-done(((bf16[1,1,1,128,1024]{4,3,2,1,0:T(8,128)(2,1)}), bf16[4,1,1,128,1024]{4,3,2,1,0:T(8,128)(2,1)}) %all-gather.2.cloned.1.call-update) | async-done | bytes 1048592 | tf_op jit(solution)/shard_map/all_gather | solution.py:59
  37.9 1.9 collective-permute-start.1
  39.8 2.4 %collective-permute-start = (bf16[4,1,1,128,1024]{4,3,0,2,1:T(8,128)(2,1)}, bf16[4,1,1,128,1024]{4,3,0,2,1:T(8,128)(2,1)S(1)}, u32[]{:S(2)}, u32[]{:S(2)}) collective-permute-start(bf16[4,1,1,128,1024]{4,3,0,2,1:T(8,128)(2,1)} %bitcast.169), channel_id=1, source_target_pairs={{0,8},{8,16},{16,24},{24,32},{32,40},{40,48},{48,56},{1,9},{9,17},... | collective-permute-start | bytes 3145736 | tf_op jit(solution)/shard_map/ppermute | solution.py:15
  42.3 21.4 %collective-permute-done.1 = bf16[4,1,1,128,1024]{4,3,0,2,1:T(8,128)(2,1)S(1)} collective-permute-done((bf16[4,1,1,128,1024]{4,3,0,2,1:T(8,128)(2,1)}, bf16[4,1,1,128,1024]{4,3,0,2,1:T(8,128)(2,1)S(1)}, u32[]{:S(2)}, u32[]{:S(2)}) %collective-permute-start.1) | collective-permute-done | bytes 1048608 | tf_op jit(solution)/shard_map/ppermute | solution.py:18
  63.7 2.3 %pad_maximum_fusion = bf16[4,3,1,128,1024]{4,3,2,1,0:T(8,128)(2,1)S(1)} fusion(bf16[4,1,1,128,1024]{4,3,2,1,0:T(8,128)(2,1)S(1)} %bitcast.170, bf16[4,1,1,128,1024]{4,3,2,1,0:T(8,128)(2,1)} %all-gather.2.cloned.1.call-done, bf16[4,1,1,128,1024]{4,3,2,1,0:T(8,128)(2,1)S(1)} %bitcast.171), kind=kLoop, calls=%fused_computation.20 | loop fusion | flops 3145728 | bytes 6291456 | tf_op jit(solution)/shard_map/concatenate | solution.py:19
  66.0 2.2 %copy.51 = bf16[4,3,1,128,1024]{4,3,0,2,1:T(8,128)(2,1)} copy(bf16[4,3,1,128,1024]{4,3,2,1,0:T(8,128)(2,1)S(1)} %pad_maximum_fusion) | data formatting | bytes 6291456 | tf_op jit(solution)/shard_map/concatenate | solution.py:19
  68.3 7.7 %collective-permute-start.2 = (bf16[4,3,1,128,1024]{4,3,0,2,1:T(8,128)(2,1)}, bf16[4,3,1,128,1024]{4,3,0,2,1:T(8,128)(2,1)}, u32[]{:S(2)}, u32[]{:S(2)}) collective-permute-start(bf16[4,3,1,128,1024]{4,3,0,2,1:T(8,128)(2,1)} %copy.51), channel_id=1, source_target_pairs={{0,1},{1,2},{2,3},{3,4},{4,5},{5,6},{6,7},{8,9},{9,10},{10,11},{11... | collective-permute-start | bytes 9437192 | tf_op jit(solution)/shard_map/ppermute | solution.py:15
  76.0 1.9 collective-permute-start.3
  77.9 1.2 copy.52
  79.1 0.7 pad_dynamic-slice_fusion.3
  79.8 1.1 fusion.100
  80.9 0.7 stack.6
  81.6 1.3 iota_compare_fusion.4
  82.9 0.7 fusion.105
  83.6 0.2 slice_reduce_fusion
  83.8 0.7 fusion.125
  84.5 0.7 compare_bitcast_fusion
  85.1 2.7 %fusion.93 = (pred[640]{0:T(1024)(128)(4,1)S(1)}, pred[640]{0:T(1024)(128)(4,1)S(1)}, pred[640]{0:T(1024)(128)(4,1)S(1)}, pred[640]{0:T(1024)(128)(4,1)S(1)}) fusion(s32[5]{0:T(128)S(1)} %get-tuple-element.12, pred[]{:T(512)} %bitcast.19, pred[5]{0:T(512)(128)(4,1)S(1)} %compare_bitcast_fusion, pred[]{:T(512)} %bitcast.26, s32[5]{0:T(128)S(1)} %get-tuple-element.11, ...), kind=kLoop, calls=%fused_computation.103 | loop fusion | flops 7680 | bytes 2649 | tf_op jit(solution)/shard_map/and | solution.py:72
  87.8 1.3 bitcast_dynamic-update-slice_fusion.2
  89.1 1.3 bitcast_dynamic-update-slice_fusion.1
  90.5 52.5 %collective-permute-done.2 = bf16[4,3,1,128,1024]{4,3,0,2,1:T(8,128)(2,1)} collective-permute-done((bf16[4,3,1,128,1024]{4,3,0,2,1:T(8,128)(2,1)}, bf16[4,3,1,128,1024]{4,3,0,2,1:T(8,128)(2,1)}, u32[]{:S(2)}, u32[]{:S(2)}) %collective-permute-start.2) | collective-permute-done | bytes 3145760 | tf_op jit(solution)/shard_map/ppermute | solution.py:15
  143.1 1.3 fusion.66
  144.4 4.7 %collective-permute-done.3 = bf16[4,3,1,128,1024]{4,3,2,1,0:T(8,128)(2,1)} collective-permute-done((bf16[4,3,1,128,1024]{4,3,2,1,0:T(8,128)(2,1)S(1)}, bf16[4,3,1,128,1024]{4,3,2,1,0:T(8,128)(2,1)}, u32[]{:S(2)}, u32[]{:S(2)}) %collective-permute-start.3) | collective-permute-done | bytes 3145760 | tf_op jit(solution)/shard_map/ppermute | solution.py:18
  149.1 1.3 fusion.65
  150.4 1.6 slice_bitcast_fusion.2
  152.0 1.2 fusion.123
  153.2 2.3 %reshape.186 = bf16[640,4,128]{2,1,0:T(4,128)(2,1)} reshape(bf16[5,128,512]{2,1,0:T(8,128)(2,1)} %get-tuple-element.29) | data formatting | bytes 1310720 | tf_op jit(solution)/shard_map/reshape | solution.py:68
  155.6 2.3 %reshape.185 = bf16[640,4,128]{2,1,0:T(4,128)(2,1)} reshape(bf16[5,128,512]{2,1,0:T(8,128)(2,1)} %get-tuple-element.30) | data formatting | bytes 1310720 | tf_op jit(solution)/shard_map/reshape | solution.py:67
  157.9 2.4 %fusion.121 = (bf16[5,128,512]{2,1,0:T(8,128)(2,1)}, bf16[5,128,512]{2,1,0:T(8,128)(2,1)}) fusion(bf16[5,128,1024]{2,1,0:T(8,128)(2,1)} %get-tuple-element.22), kind=kLoop, calls=%fused_computation.133 | loop fusion | bytes 2621440 | tf_op jit(solution)/shard_map/slice | solution.py:68
  160.4 2.3 %reshape.190 = bf16[640,4,128]{2,1,0:T(4,128)(2,1)} reshape(bf16[5,128,512]{2,1,0:T(8,128)(2,1)} %get-tuple-element.25) | data formatting | bytes 1310720 | tf_op jit(solution)/shard_map/reshape | solution.py:68
  162.7 2.3 %reshape.189 = bf16[640,4,128]{2,1,0:T(4,128)(2,1)} reshape(bf16[5,128,512]{2,1,0:T(8,128)(2,1)} %get-tuple-element.26) | data formatting | bytes 1310720 | tf_op jit(solution)/shard_map/reshape | solution.py:67
  165.0 1.2 fusion.122
  166.2 2.3 %reshape.188 = bf16[640,4,128]{2,1,0:T(4,128)(2,1)} reshape(bf16[5,128,512]{2,1,0:T(8,128)(2,1)} %get-tuple-element.27) | data formatting | bytes 1310720 | tf_op jit(solution)/shard_map/reshape | solution.py:68
  168.5 2.3 %reshape.187 = bf16[640,4,128]{2,1,0:T(4,128)(2,1)} reshape(bf16[5,128,512]{2,1,0:T(8,128)(2,1)} %get-tuple-element.28) | data formatting | bytes 1310720 | tf_op jit(solution)/shard_map/reshape | solution.py:67
  171.0 1.0 reshape.184
  172.0 0.2 reshape.182
  172.1 0.8 bitcast_reduce_fusion.3
  173.0 0.8 bitcast_reduce_fusion.1
  173.8 0.8 bitcast_reduce_fusion
  174.6 0.8 bitcast_reduce_fusion.2
  175.4 2.5 %fusion.8 = (f32[128,4,3]{0,2,1:T(4,128)S(1)}, f32[128,4,3]{0,2,1:T(4,128)S(1)}) fusion(f32[4,640,128,3]{2,1,3,0:T(8,128)S(1)} %get-tuple-element.50, f32[128,4,3]{0,2,1:T(4,128)S(1)} %get-tuple-element.34, pred[640]{0:T(1024)(128)(4,1)S(1)} %get-tuple-element.38, f32[128,4,3]{0,2,1:T(4,128)S(1)} %get-tuple-element.20, ...), kind=kLoop, calls=%fused_computation.21 | loop fusion | flops 9827328 | bytes 7890176 | tf_op jit(solution)/shard_map/reduce_sum | solution.py:82
  178.0 2.7 %fusion.12 = (f32[128,4,3]{0,2,1:T(4,128)S(1)}, f32[128,4,3]{0,2,1:T(4,128)S(1)}) fusion(f32[4,640,128,3]{2,1,3,0:T(8,128)S(1)} %get-tuple-element.46, f32[128,4,3]{0,2,1:T(4,128)S(1)} %get-tuple-element.19, pred[640]{0:T(1024)(128)(4,1)S(1)} %get-tuple-element.36, f32[128,4,3]{0,2,1:T(4,128)S(1)} %get-tuple-element.18, ...), kind=kLoop, calls=%fused_computation.25 | loop fusion | flops 9827328 | bytes 7890176 | tf_op jit(solution)/shard_map/reduce_sum | solution.py:82
  180.8 1.4 fusion.56
  182.1 1.4 fusion.59
  183.5 1.4 fusion.62
  184.9 1.4 fusion.73
  186.3 0.9 copy.69
  (30 shorter events, 0.3 us)
Async XLA Ops:
  6.5 31.4 %all-gather.2.cloned.1.call-start = ((), (), s32[]{:S(2)}) async-start(), calls=%async_computation | async-start | bytes 1310720 | tf_op jit(solution)/shard_map/all_gather | solution.py:59
  37.9 25.8 %collective-permute-start.1 = (bf16[4,1,1,128,1024]{4,3,0,2,1:T(8,128)(2,1)}, bf16[4,1,1,128,1024]{4,3,0,2,1:T(8,128)(2,1)S(1)}, u32[]{:S(2)}, u32[]{:S(2)}) collective-permute-start(bf16[4,1,1,128,1024]{4,3,0,2,1:T(8,128)(2,1)} %bitcast.168), channel_id=1, source_target_pairs={{8,0},{16,8},{24,16},{32,24},{40,32},{48,40},{56,48},{9,1},{17,9},... | collective-permute-start | bytes 3145736 | tf_op jit(solution)/shard_map/ppermute | solution.py:18
  39.8 23.9 %collective-permute-start = (bf16[4,1,1,128,1024]{4,3,0,2,1:T(8,128)(2,1)}, bf16[4,1,1,128,1024]{4,3,0,2,1:T(8,128)(2,1)S(1)}, u32[]{:S(2)}, u32[]{:S(2)}) collective-permute-start(bf16[4,1,1,128,1024]{4,3,0,2,1:T(8,128)(2,1)} %bitcast.169), channel_id=1, source_target_pairs={{0,8},{8,16},{16,24},{24,32},{32,40},{40,48},{48,56},{1,9},{9,17},... | collective-permute-start | bytes 3145736 | tf_op jit(solution)/shard_map/ppermute | solution.py:15
  63.7 4.6 %copy-start = (bf16[4,1,1,128,1024]{4,3,0,2,1:T(8,128)(2,1)}, bf16[4,1,1,128,1024]{4,3,0,2,1:T(8,128)(2,1)S(1)}, u32[]{:S(2)}) copy-start(bf16[4,1,1,128,1024]{4,3,0,2,1:T(8,128)(2,1)S(1)} %collective-permute-done.1) | copy-start | bytes 3145732
  63.7 4.6 %copy-start.2 = (bf16[4,1,1,128,1024]{4,3,0,2,1:T(8,128)(2,1)}, bf16[4,1,1,128,1024]{4,3,0,2,1:T(8,128)(2,1)S(1)}, u32[]{:S(2)}) copy-start(bf16[4,1,1,128,1024]{4,3,0,2,1:T(8,128)(2,1)S(1)} %collective-permute-done) | copy-start | bytes 3145732
  66.0 13.1 %copy-start.10 = (s32[4,8,8]{2,1,0:T(8,128)S(1)}, s32[4,8,8]{2,1,0:T(8,128)}, u32[]{:S(2)}) copy-start(s32[4,8,8]{2,1,0:T(8,128)} %param.8) | copy-start | bytes 3076
  68.3 74.8 %collective-permute-start.2 = (bf16[4,3,1,128,1024]{4,3,0,2,1:T(8,128)(2,1)}, bf16[4,3,1,128,1024]{4,3,0,2,1:T(8,128)(2,1)}, u32[]{:S(2)}, u32[]{:S(2)}) collective-permute-start(bf16[4,3,1,128,1024]{4,3,0,2,1:T(8,128)(2,1)} %copy.51), channel_id=1, source_target_pairs={{0,1},{1,2},{2,3},{3,4},{4,5},{5,6},{6,7},{8,9},{9,10},{10,11},{11... | collective-permute-start | bytes 9437192 | tf_op jit(solution)/shard_map/ppermute | solution.py:15
  76.0 73.1 %collective-permute-start.3 = (bf16[4,3,1,128,1024]{4,3,2,1,0:T(8,128)(2,1)S(1)}, bf16[4,3,1,128,1024]{4,3,2,1,0:T(8,128)(2,1)}, u32[]{:S(2)}, u32[]{:S(2)}) collective-permute-start(bf16[4,3,1,128,1024]{4,3,2,1,0:T(8,128)(2,1)S(1)} %pad_maximum_fusion), channel_id=1, source_target_pairs={{1,0},{2,1},{3,2},{4,3},{5,4},{6,5},{7,6},{9,8},{10,9},{11,10},{12... | collective-permute-start | bytes 9437192 | tf_op jit(solution)/shard_map/ppermute | solution.py:18
  81.6 8.8 %copy-start.1 = (bf16[4,1,1,128,1024]{4,3,0,2,1:T(8,128)(2,1)S(1)}, bf16[4,1,1,128,1024]{4,3,0,2,1:T(8,128)(2,1)}, u32[]{:S(2)}) copy-start(bf16[4,1,1,128,1024]{4,3,0,2,1:T(8,128)(2,1)} %copy-done) | copy-start | bytes 3145732
  171.0 2.0 %copy-start.5 = (bf16[640,4,128]{2,1,0:T(4,128)(2,1)S(1)}, bf16[640,4,128]{2,1,0:T(4,128)(2,1)}, u32[]{:S(2)}) copy-start(bf16[640,4,128]{2,1,0:T(4,128)(2,1)} %reshape.187) | copy-start | bytes 1966084
  172.1 1.6 copy-start.4
  173.0 1.6 copy-start.3
  178.0 2.8 %copy-start.9 = (bf16[640,4,128]{2,1,0:T(4,128)(2,1)S(1)}, bf16[640,4,128]{2,1,0:T(4,128)(2,1)}, u32[]{:S(2)}) copy-start(bf16[640,4,128]{2,1,0:T(4,128)(2,1)} %reshape.184) | copy-start | bytes 1966084
  180.8 1.4 copy-start.7
  182.1 1.4 copy-start.8
  183.5 1.4 copy-start.6
  183.5 1.4 copy-start.11
Sparse Core Ops, SparseCore 0:
  9.2 28.7 all-gather.1
where the time goes:
time: 195 us; the launch traced here: 194 us
  waiting for transfers between devices  110 us (56%)
  local copies, waits for them, and re-layouts  34.7 us (18%)
  starting transfers between devices  13.9 us (7%)
  between operations  13.7 us (7%)
  other arithmetic  13 us (7%)
  matrix products  8.64 us (4%)
    ppermute x2, waiting for transfers between devices, padded(): lax.ppermute(lax.slice_in_dim(block, block.shape[dim] - width, None, axis...  52.5 us
    all_gather x1, waiting for transfers between devices, shards(): cached = lax.all_gather(key_value, 'span', axis=0, tiled=True)  30.7 us
    ppermute x2, waiting for transfers between devices, padded(): lax.ppermute(lax.slice_in_dim(block, 0, width, axis=dim), axis, backward)  26.2 us
    ppermute x2, starting transfers between devices, padded(): lax.ppermute(lax.slice_in_dim(block, block.shape[dim] - width, None, axis...  10.1 us
    reshape x4, local copies, waits for them, and re-layouts, shards(): key_value_block[:, :, kv_width:].reshape(-1, kv_heads, HEAD_SIZE)  7.99 us
    reshape x4, local copies, waits for them, and re-layouts, shards(): key_value_block[:, :, :kv_width].reshape(-1, kv_heads, HEAD_SIZE)  7.14 us
    dot_general x4, matrix products, shards(): jnp.einsum('tkgl,lkd->tkgd', weights.astype(jnp.bfloat16), value_rows, pr...  5.44 us
    reduce_sum x2, other arithmetic, shards(): attend_run_sum = attend_run_sum * fade_factor + jnp.sum(weights, axis=-1)  5.27 us
  transfers between devices with their start and end apart: 5, of which 4 were waited for; matrix products, arithmetic and copies ran while one was open for 7% of the time, Pallas kernels for 0%

commit v1 on v0

--- a/solution.py
+++ b/solution.py
@@ -5,6 +5,19 @@
 
 HEAD_SIZE = 128
 NEIGH = 5
+
+
+def collect(x, axis, dim):
+    ways = lax.axis_size(axis)
+    up = [(d, (d + 1) % ways) for d in range(ways)]
+    down = [(d, (d - 1) % ways) for d in range(ways)]
+    earlier, later = ([x], [x])
+    for _ in range(ways // 2):
+        earlier.append(lax.ppermute(earlier[-1], axis, up))
+    for _ in range((ways - 1) // 2):
+        later.append(lax.ppermute(later[-1], axis, down))
+    line = jnp.concatenate([*earlier[::-1], *later[1:]], axis=dim)
+    return jnp.roll(line, (lax.axis_index(axis) - ways // 2) * x.shape[dim], axis=dim)
 
 
 def padded(block, sides, width):
@@ -56,7 +69,7 @@
         jnp.zeros((tok_rows, kv_heads, groups), jnp.float32),
         jnp.zeros((tok_rows, kv_heads, groups, HEAD_SIZE), jnp.float32),
     )
-    cached = lax.all_gather(key_value, "span", axis=0, tiled=True)
+    cached = collect(key_value, "span", 0)
     extended = padded(cached, (("ty", 1), ("tx", 2)), 1)
     state_now = initial
     kv_piece = cross_tiles(extended)

time: 195 us -> 174 us (0.89)
  waiting for transfers between devices: 110 us -> 89.3 us
  between operations: 13.7 us -> 0.35 us
  local copies, waits for them, and re-layouts: 34.7 us -> 44.9 us
  starting transfers between devices: 13.9 us -> 19.3 us
  other arithmetic: 13 us -> 10.9 us
    all_gather x1 -> x0, waiting for transfers between devices: 30.7 us -> none  [shards(): cached = lax.all_gather(key_value, 'span', axis=0, tiled=True)]
    ppermute x0 -> x3, waiting for transfers between devices: none -> 13.2 us  [the longest x2 13.2 us: collect(): earlier.append(lax.ppermute(earlier[-1], axis, up))]
    unnamed x29 -> x34, local copies, waits for them, and re-layouts: 5.22 us -> 11.5 us
    ppermute x0 -> x3, starting transfers between devices: none -> 4.81 us  [the longest x1 2.93 us: collect(): later.append(lax.ppermute(later[-1], axis, down))]
    squeeze x1, local copies, waits for them, and re-layouts: 1.64 us -> 4.42 us  [shards(): key_value_block = kv_piece[offset]]
    concatenate x1, other arithmetic: 2.32 us -> 0.34 us  [padded(): block = jnp.concatenate([low, block, high], axis=dim)]
  transfers between devices with their start and end apart: 5 -> 7, of which waited for: 4 -> 5; matrix products, arithmetic and copies ran while one was open for 7% -> 10% of each run, Pallas kernels for 0% -> 0%
where the time goes in v1:
time: 174 us; the launch traced here: 173 us
  waiting for transfers between devices  89.3 us (51%)
  local copies, waits for them, and re-layouts  44.9 us (26%)
  starting transfers between devices  19.3 us (11%)
  other arithmetic  10.9 us (6%)
  matrix products  8.65 us (5%)
    ppermute x2, waiting for transfers between devices, padded(): lax.ppermute(lax.slice_in_dim(block, block.shape[dim] - width, None, axis...  51.3 us
    ppermute x2, waiting for transfers between devices, padded(): lax.ppermute(lax.slice_in_dim(block, 0, width, axis=dim), axis, backward)  24.9 us
    ppermute x2, waiting for transfers between devices, collect(): earlier.append(lax.ppermute(earlier[-1], axis, up))  13.2 us
    unnamed x34, local copies, waits for them, and re-layouts  11.5 us
    ppermute x2, starting transfers between devices, padded(): lax.ppermute(lax.slice_in_dim(block, block.shape[dim] - width, None, axis...  10.5 us
    reshape x4, local copies, waits for them, and re-layouts, shards(): key_value_block[:, :, kv_width:].reshape(-1, kv_heads, HEAD_SIZE)  7.99 us
    reshape x4, local copies, waits for them, and re-layouts, shards(): key_value_block[:, :, :kv_width].reshape(-1, kv_heads, HEAD_SIZE)  7.14 us
    dot_general x4, matrix products, shards(): jnp.einsum('tkgl,lkd->tkgd', weights.astype(jnp.bfloat16), value_rows, pr...  5.44 us
  transfers between devices with their start and end apart: 7, of which 5 were waited for; matrix products, arithmetic and copies ran while one was open for 10% of the time, Pallas kernels for 0%

profile of v1, /device:TPU:70, one launch (start us, length us, event | category | flops | bytes accessed | tf_op | source)
XLA Modules:
  0.0 173.4 jit_solution(11767075773684551344)
XLA Ops:
  0.0 1.6 collective-permute-start
  1.6 8.0 %collective-permute-done = bf16[1,1,1,128,1024]{4,3,2,1,0:T(8,128)(2,1)S(1)} collective-permute-done((bf16[1,1,1,128,1024]{4,3,2,1,0:T(8,128)(2,1)}, bf16[1,1,1,128,1024]{4,3,2,1,0:T(8,128)(2,1)S(1)}, u32[]{:S(2)}, u32[]{:S(2)}) %collective-permute-start) | collective-permute-done | bytes 262176 | tf_op jit(solution)/shard_map/ppermute | solution.py:16
  9.8 2.9 %collective-permute-start.2 = (bf16[1,1,1,128,1024]{4,3,2,1,0:T(8,128)(2,1)}, bf16[1,1,1,128,1024]{4,3,2,1,0:T(8,128)(2,1)S(1)}, u32[]{:S(2)}, u32[]{:S(2)}) collective-permute-start(bf16[1,1,1,128,1024]{4,3,2,1,0:T(8,128)(2,1)} %param.6), channel_id=1, source_target_pairs={{0,192},{64,0},{128,64},{192,128},{1,193},{65,1},{129,65},{193,129... | collective-permute-start | bytes 786440 | tf_op jit(solution)/shard_map/ppermute | solution.py:18
  12.8 5.2 %collective-permute-done.1 = bf16[1,1,1,128,1024]{4,3,2,1,0:T(8,128)(2,1)S(1)} collective-permute-done((bf16[1,1,1,128,1024]{4,3,2,1,0:T(8,128)(2,1)S(1)}, bf16[1,1,1,128,1024]{4,3,2,1,0:T(8,128)(2,1)S(1)}, u32[]{:S(2)}, u32[]{:S(2)}) %collective-permute-start.1) | collective-permute-done | bytes 262176 | tf_op jit(solution)/shard_map/ppermute | solution.py:16
  18.0 1.0 constant_dynamic-update-slice_fusion.5
  19.1 1.0 constant_dynamic-update-slice_fusion.1
  20.1 1.3 bitcast_dynamic-update-slice_fusion.2
  21.4 1.9 %collective-permute-start.4 = (bf16[4,1,1,128,1024]{4,3,0,2,1:T(8,128)(2,1)S(1)}, bf16[4,1,1,128,1024]{4,3,0,2,1:T(8,128)(2,1)S(1)}, u32[]{:S(2)}, u32[]{:S(2)}) collective-permute-start(bf16[4,1,1,128,1024]{4,3,0,2,1:T(8,128)(2,1)S(1)} %bitcast.170), channel_id=1, source_target_pairs={{8,0},{16,8},{24,16},{32,24},{40,32},{48,40},{56,48},{9,1},{17,9},... | collective-permute-start | bytes 3145736 | tf_op jit(solution)/shard_map/ppermute | solution.py:31
  23.3 2.4 %collective-permute-start.3 = (bf16[4,1,1,128,1024]{4,3,0,2,1:T(8,128)(2,1)S(1)}, bf16[4,1,1,128,1024]{4,3,0,2,1:T(8,128)(2,1)S(1)}, u32[]{:S(2)}, u32[]{:S(2)}) collective-permute-start(bf16[4,1,1,128,1024]{4,3,0,2,1:T(8,128)(2,1)S(1)} %bitcast.171), channel_id=1, source_target_pairs={{0,8},{8,16},{16,24},{24,32},{32,40},{40,48},{48,56},{1,9},{9,17},... | collective-permute-start | bytes 3145736 | tf_op jit(solution)/shard_map/ppermute | solution.py:28
  25.8 21.1 %collective-permute-done.4 = bf16[4,1,1,128,1024]{4,3,0,2,1:T(8,128)(2,1)S(1)} collective-permute-done((bf16[4,1,1,128,1024]{4,3,0,2,1:T(8,128)(2,1)S(1)}, bf16[4,1,1,128,1024]{4,3,0,2,1:T(8,128)(2,1)S(1)}, u32[]{:S(2)}, u32[]{:S(2)}) %collective-permute-start.4) | collective-permute-done | bytes 1048608 | tf_op jit(solution)/shard_map/ppermute | solution.py:31
  47.2 2.3 %copy.28 = bf16[4,3,1,128,1024]{4,3,0,2,1:T(8,128)(2,1)} copy(bf16[4,3,1,128,1024]{4,3,2,1,0:T(8,128)(2,1)S(1)} %pad_maximum_fusion) | data formatting | bytes 6291456 | tf_op jit(solution)/shard_map/concatenate | solution.py:32
  49.6 8.1 %collective-permute-start.5 = (bf16[4,3,1,128,1024]{4,3,0,2,1:T(8,128)(2,1)}, bf16[4,3,1,128,1024]{4,3,0,2,1:T(8,128)(2,1)}, u32[]{:S(2)}, u32[]{:S(2)}) collective-permute-start(bf16[4,3,1,128,1024]{4,3,0,2,1:T(8,128)(2,1)} %copy.28), channel_id=1, source_target_pairs={{0,1},{1,2},{2,3},{3,4},{4,5},{5,6},{6,7},{8,9},{9,10},{10,11},{11... | collective-permute-start | bytes 9437192 | tf_op jit(solution)/shard_map/ppermute | solution.py:28
  57.7 2.1 %collective-permute-start.6 = (bf16[4,3,1,128,1024]{4,3,2,1,0:T(8,128)(2,1)S(1)}, bf16[4,3,1,128,1024]{4,3,2,1,0:T(8,128)(2,1)}, u32[]{:S(2)}, u32[]{:S(2)}) collective-permute-start(bf16[4,3,1,128,1024]{4,3,2,1,0:T(8,128)(2,1)S(1)} %pad_maximum_fusion), channel_id=1, source_target_pairs={{1,0},{2,1},{3,2},{4,3},{5,4},{6,5},{7,6},{9,8},{10,9},{11,10},{12... | collective-permute-start | bytes 9437192 | tf_op jit(solution)/shard_map/ppermute | solution.py:31
  59.8 1.2 copy.29
  61.0 0.7 pad_dynamic-slice_fusion.3
  61.7 1.1 fusion.100
  62.8 0.7 stack.6
  63.5 1.2 iota_compare_fusion.4
  64.7 0.7 fusion.105
  66.9 2.6 %fusion.93 = (pred[640]{0:T(1024)(128)(4,1)S(1)}, pred[640]{0:T(1024)(128)(4,1)S(1)}, pred[640]{0:T(1024)(128)(4,1)S(1)}, pred[640]{0:T(1024)(128)(4,1)S(1)}) fusion(s32[5]{0:T(128)S(1)} %get-tuple-element.12, pred[]{:T(512)} %bitcast.19, pred[5]{0:T(512)(128)(4,1)S(1)} %compare_bitcast_fusion, pred[]{:T(512)} %bitcast.26, s32[5]{0:T(128)S(1)} %get-tuple-element.11, ...), kind=kLoop, calls=%fused_computation.111 | loop fusion | flops 7680 | bytes 2649 | tf_op jit(solution)/shard_map/and | solution.py:85
  69.5 2.3 %bitcast_dynamic-update-slice_fusion.1 = bf16[4,5,128,1024]{3,2,0,1:T(8,128)(2,1)} fusion(bf16[4,5,128,1024]{3,2,0,1:T(8,128)(2,1)} %get-tuple-element.21, bf16[4,1,1,128,1024]{4,3,0,2,1:T(8,128)(2,1)} %copy-done.1), kind=kLoop, calls=%fused_computation.61 | loop fusion | bytes 2097152
  71.9 2.3 %bitcast_dynamic-update-slice_fusion = bf16[4,5,128,1024]{3,2,0,1:T(8,128)(2,1)} fusion(bf16[4,5,128,1024]{3,2,0,1:T(8,128)(2,1)} %bitcast_dynamic-update-slice_fusion.1, bf16[4,1,1,128,1024]{4,3,0,2,1:T(8,128)(2,1)} %copy-done), kind=kLoop, calls=%fused_computation.60 | loop fusion | bytes 2097152
  74.2 51.3 %collective-permute-done.5 = bf16[4,3,1,128,1024]{4,3,0,2,1:T(8,128)(2,1)} collective-permute-done((bf16[4,3,1,128,1024]{4,3,0,2,1:T(8,128)(2,1)}, bf16[4,3,1,128,1024]{4,3,0,2,1:T(8,128)(2,1)}, u32[]{:S(2)}, u32[]{:S(2)}) %collective-permute-start.5) | collective-permute-done | bytes 3145760 | tf_op jit(solution)/shard_map/ppermute | solution.py:28
  125.5 2.3 %fusion.66 = bf16[4,5,128,1024]{3,2,0,1:T(8,128)(2,1)} fusion(bf16[4,5,128,1024]{3,2,0,1:T(8,128)(2,1)} %bitcast_dynamic-update-slice_fusion, bf16[4,3,1,128,1024]{4,3,0,2,1:T(8,128)(2,1)} %collective-permute-done.5), kind=kLoop, calls=%fused_computation.59 | loop fusion | bytes 2097152
  127.7 3.7 %collective-permute-done.6 = bf16[4,3,1,128,1024]{4,3,2,1,0:T(8,128)(2,1)} collective-permute-done((bf16[4,3,1,128,1024]{4,3,2,1,0:T(8,128)(2,1)S(1)}, bf16[4,3,1,128,1024]{4,3,2,1,0:T(8,128)(2,1)}, u32[]{:S(2)}, u32[]{:S(2)}) %collective-permute-start.6) | collective-permute-done | bytes 3145760 | tf_op jit(solution)/shard_map/ppermute | solution.py:31
  131.5 2.3 %fusion.65 = bf16[4,5,128,1024]{3,2,0,1:T(8,128)(2,1)} fusion(bf16[4,5,128,1024]{3,2,0,1:T(8,128)(2,1)} %fusion.66, bf16[4,3,1,128,1024]{4,3,2,1,0:T(8,128)(2,1)} %collective-permute-done.6), kind=kLoop, calls=%fused_computation.57 | loop fusion | bytes 2097152 | tf_op jit(solution)/shard_map/stack | solution.py:37
  133.7 4.4 %slice_bitcast_fusion.2 = (bf16[5,128,1024]{2,1,0:T(8,128)(2,1)S(1)}, bf16[5,128,1024]{2,1,0:T(8,128)(2,1)}, bf16[5,128,1024]{2,1,0:T(8,128)(2,1)S(1)}, bf16[5,128,1024]{2,1,0:T(8,128)(2,1)S(1)}) fusion(bf16[4,5,128,1024]{3,2,0,1:T(8,128)(2,1)} %fusion.65), kind=kLoop, calls=%fused_computation.43 | loop fusion | bytes 10485760 | tf_op jit(solution)/shard_map/squeeze | solution.py:77
  138.2 1.2 fusion.123
  139.4 2.3 %reshape.186 = bf16[640,4,128]{2,1,0:T(4,128)(2,1)} reshape(bf16[5,128,512]{2,1,0:T(8,128)(2,1)} %get-tuple-element.31) | data formatting | bytes 1310720 | tf_op jit(solution)/shard_map/reshape | solution.py:81
  141.7 2.3 %reshape.185 = bf16[640,4,128]{2,1,0:T(4,128)(2,1)} reshape(bf16[5,128,512]{2,1,0:T(8,128)(2,1)} %get-tuple-element.32) | data formatting | bytes 1310720 | tf_op jit(solution)/shard_map/reshape | solution.py:80
  144.0 2.4 %fusion.121 = (bf16[5,128,512]{2,1,0:T(8,128)(2,1)}, bf16[5,128,512]{2,1,0:T(8,128)(2,1)}) fusion(bf16[5,128,1024]{2,1,0:T(8,128)(2,1)} %get-tuple-element.24), kind=kLoop, calls=%fused_computation.142 | loop fusion | bytes 2621440 | tf_op jit(solution)/shard_map/slice | solution.py:81
  146.5 2.3 %reshape.190 = bf16[640,4,128]{2,1,0:T(4,128)(2,1)} reshape(bf16[5,128,512]{2,1,0:T(8,128)(2,1)} %get-tuple-element.27) | data formatting | bytes 1310720 | tf_op jit(solution)/shard_map/reshape | solution.py:81
  148.8 2.3 %reshape.189 = bf16[640,4,128]{2,1,0:T(4,128)(2,1)} reshape(bf16[5,128,512]{2,1,0:T(8,128)(2,1)} %get-tuple-element.28) | data formatting | bytes 1310720 | tf_op jit(solution)/shard_map/reshape | solution.py:80
  151.2 1.2 fusion.122
  152.4 2.3 %reshape.188 = bf16[640,4,128]{2,1,0:T(4,128)(2,1)} reshape(bf16[5,128,512]{2,1,0:T(8,128)(2,1)} %get-tuple-element.29) | data formatting | bytes 1310720 | tf_op jit(solution)/shard_map/reshape | solution.py:81
  154.7 2.3 %reshape.187 = bf16[640,4,128]{2,1,0:T(4,128)(2,1)} reshape(bf16[5,128,512]{2,1,0:T(8,128)(2,1)} %get-tuple-element.30) | data formatting | bytes 1310720 | tf_op jit(solution)/shard_map/reshape | solution.py:80
  157.1 1.0 reshape.184
  158.3 0.8 bitcast_reduce_fusion.3
  159.1 0.8 bitcast_reduce_fusion.1
  159.9 0.8 bitcast_reduce_fusion
  160.8 0.8 bitcast_reduce_fusion.2
  161.6 2.5 %fusion.8 = (f32[128,4,3]{0,2,1:T(4,128)S(1)}, f32[128,4,3]{0,2,1:T(4,128)S(1)}) fusion(f32[4,640,128,3]{2,1,3,0:T(8,128)S(1)} %get-tuple-element.52, f32[128,4,3]{0,2,1:T(4,128)S(1)} %get-tuple-element.36, pred[640]{0:T(1024)(128)(4,1)S(1)} %get-tuple-element.40, f32[128,4,3]{0,2,1:T(4,128)S(1)} %get-tuple-element.20, ...), kind=kLoop, calls=%fused_computation.21 | loop fusion | flops 9827328 | bytes 7890176 | tf_op jit(solution)/shard_map/reduce_sum | solution.py:95
  164.1 2.8 %fusion.12 = (f32[128,4,3]{0,2,1:T(4,128)S(1)}, f32[128,4,3]{0,2,1:T(4,128)S(1)}) fusion(f32[4,640,128,3]{2,1,3,0:T(8,128)S(1)} %get-tuple-element.48, f32[128,4,3]{0,2,1:T(4,128)S(1)} %get-tuple-element.19, pred[640]{0:T(1024)(128)(4,1)S(1)} %get-tuple-element.38, f32[128,4,3]{0,2,1:T(4,128)S(1)} %get-tuple-element.18, ...), kind=kLoop, calls=%fused_computation.25 | loop fusion | flops 9827328 | bytes 7890176 | tf_op jit(solution)/shard_map/reduce_sum | solution.py:95
  167.0 1.4 fusion.56
  168.3 1.4 fusion.59
  169.7 1.4 fusion.62
  171.1 1.4 fusion.73
  172.5 0.9 copy.46
  (39 shorter events, 2.7 us)
Async XLA Ops:
  0.0 9.5 %collective-permute-start = (bf16[1,1,1,128,1024]{4,3,2,1,0:T(8,128)(2,1)}, bf16[1,1,1,128,1024]{4,3,2,1,0:T(8,128)(2,1)S(1)}, u32[]{:S(2)}, u32[]{:S(2)}) collective-permute-start(bf16[1,1,1,128,1024]{4,3,2,1,0:T(8,128)(2,1)} %param.6), channel_id=1, source_target_pairs={{0,64},{64,128},{128,192},{192,0},{1,65},{65,129},{129,193},{193,1... | collective-permute-start | bytes 786440 | tf_op jit(solution)/shard_map/ppermute | solution.py:16
  9.5 8.5 %collective-permute-start.1 = (bf16[1,1,1,128,1024]{4,3,2,1,0:T(8,128)(2,1)S(1)}, bf16[1,1,1,128,1024]{4,3,2,1,0:T(8,128)(2,1)S(1)}, u32[]{:S(2)}, u32[]{:S(2)}) collective-permute-start(bf16[1,1,1,128,1024]{4,3,2,1,0:T(8,128)(2,1)S(1)} %collective-permute-done), channel_id=1, source_target_pairs={{0,64},{64,128},{128,192},{192,0},{1,65},{65,129},{129,193},{193,1... | collective-permute-start | bytes 786440 | tf_op jit(solution)/shard_map/ppermute | solution.py:16
  9.8 9.2 %collective-permute-start.2 = (bf16[1,1,1,128,1024]{4,3,2,1,0:T(8,128)(2,1)}, bf16[1,1,1,128,1024]{4,3,2,1,0:T(8,128)(2,1)S(1)}, u32[]{:S(2)}, u32[]{:S(2)}) collective-permute-start(bf16[1,1,1,128,1024]{4,3,2,1,0:T(8,128)(2,1)} %param.6), channel_id=1, source_target_pairs={{0,192},{64,0},{128,64},{192,128},{1,193},{65,1},{129,65},{193,129... | collective-permute-start | bytes 786440 | tf_op jit(solution)/shard_map/ppermute | solution.py:18
  21.4 25.4 %collective-permute-start.4 = (bf16[4,1,1,128,1024]{4,3,0,2,1:T(8,128)(2,1)S(1)}, bf16[4,1,1,128,1024]{4,3,0,2,1:T(8,128)(2,1)S(1)}, u32[]{:S(2)}, u32[]{:S(2)}) collective-permute-start(bf16[4,1,1,128,1024]{4,3,0,2,1:T(8,128)(2,1)S(1)} %bitcast.170), channel_id=1, source_target_pairs={{8,0},{16,8},{24,16},{32,24},{40,32},{48,40},{56,48},{9,1},{17,9},... | collective-permute-start | bytes 3145736 | tf_op jit(solution)/shard_map/ppermute | solution.py:31
  23.3 23.5 %collective-permute-start.3 = (bf16[4,1,1,128,1024]{4,3,0,2,1:T(8,128)(2,1)S(1)}, bf16[4,1,1,128,1024]{4,3,0,2,1:T(8,128)(2,1)S(1)}, u32[]{:S(2)}, u32[]{:S(2)}) collective-permute-start(bf16[4,1,1,128,1024]{4,3,0,2,1:T(8,128)(2,1)S(1)} %bitcast.171), channel_id=1, source_target_pairs={{0,8},{8,16},{16,24},{24,32},{32,40},{40,48},{48,56},{1,9},{9,17},... | collective-permute-start | bytes 3145736 | tf_op jit(solution)/shard_map/ppermute | solution.py:28
  46.9 2.7 %copy-start = (bf16[4,1,1,128,1024]{4,3,0,2,1:T(8,128)(2,1)}, bf16[4,1,1,128,1024]{4,3,0,2,1:T(8,128)(2,1)S(1)}, u32[]{:S(2)}) copy-start(bf16[4,1,1,128,1024]{4,3,0,2,1:T(8,128)(2,1)S(1)} %collective-permute-done.4) | copy-start | bytes 3145732
  46.9 2.7 %copy-start.1 = (bf16[4,1,1,128,1024]{4,3,0,2,1:T(8,128)(2,1)}, bf16[4,1,1,128,1024]{4,3,0,2,1:T(8,128)(2,1)S(1)}, u32[]{:S(2)}) copy-start(bf16[4,1,1,128,1024]{4,3,0,2,1:T(8,128)(2,1)S(1)} %collective-permute-done.3) | copy-start | bytes 3145732
  47.2 13.8 %copy-start.9 = (s32[4,8,8]{2,1,0:T(8,128)S(1)}, s32[4,8,8]{2,1,0:T(8,128)}, u32[]{:S(2)}) copy-start(s32[4,8,8]{2,1,0:T(8,128)} %param.8) | copy-start | bytes 3076
  49.6 75.9 %collective-permute-start.5 = (bf16[4,3,1,128,1024]{4,3,0,2,1:T(8,128)(2,1)}, bf16[4,3,1,128,1024]{4,3,0,2,1:T(8,128)(2,1)}, u32[]{:S(2)}, u32[]{:S(2)}) collective-permute-start(bf16[4,3,1,128,1024]{4,3,0,2,1:T(8,128)(2,1)} %copy.28), channel_id=1, source_target_pairs={{0,1},{1,2},{2,3},{3,4},{4,5},{5,6},{6,7},{8,9},{9,10},{10,11},{11... | collective-permute-start | bytes 9437192 | tf_op jit(solution)/shard_map/ppermute | solution.py:28
  57.7 73.8 %collective-permute-start.6 = (bf16[4,3,1,128,1024]{4,3,2,1,0:T(8,128)(2,1)S(1)}, bf16[4,3,1,128,1024]{4,3,2,1,0:T(8,128)(2,1)}, u32[]{:S(2)}, u32[]{:S(2)}) collective-permute-start(bf16[4,3,1,128,1024]{4,3,2,1,0:T(8,128)(2,1)S(1)} %pad_maximum_fusion), channel_id=1, source_target_pairs={{1,0},{2,1},{3,2},{4,3},{5,4},{6,5},{7,6},{9,8},{10,9},{11,10},{12... | collective-permute-start | bytes 9437192 | tf_op jit(solution)/shard_map/ppermute | solution.py:31
  157.1 2.0 %copy-start.4 = (bf16[640,4,128]{2,1,0:T(4,128)(2,1)S(1)}, bf16[640,4,128]{2,1,0:T(4,128)(2,1)}, u32[]{:S(2)}) copy-start(bf16[640,4,128]{2,1,0:T(4,128)(2,1)} %reshape.187) | copy-start | bytes 1966084
  158.3 1.6 copy-start.3
  159.1 1.6 copy-start.2
  164.1 2.8 %copy-start.8 = (bf16[640,4,128]{2,1,0:T(4,128)(2,1)S(1)}, bf16[640,4,128]{2,1,0:T(4,128)(2,1)}, u32[]{:S(2)}) copy-start(bf16[640,4,128]{2,1,0:T(4,128)(2,1)} %reshape.184) | copy-start | bytes 1966084
  167.0 1.4 copy-start.6
  168.3 1.4 copy-start.7
  169.7 1.4 copy-start.5
  169.7 1.4 copy-start.10
